TPU v7x, 32 devices: a whole 2x2x4 slice. The times are simulated.
32 devices in a mesh: dp: 16 (over z, x, core), tensor: 2 (over y).
Axes of the slice: x: 2, y: 2, z: 4, core: 2. Of those that a mesh axis runs over, the one named last changes fastest.
Arguments:
- tokens: bfloat16 [6144, 2048], P(('dp', 'tensor')), may hold values from -6 to 6
- routes: int32 [6144, 8], P('dp'), may hold values from 0 to 15, all different within a row; in each aligned block of 192 rows (0 to 191, 192 to 383, ...) at most 128 rows name the same one
- cotangent: bfloat16 [6144, 2048], P(('dp', 'tensor')), may hold values from -6 to 6
- attn_gain: float32 [2048], replicated, may hold values from 0.5 to 1.5
- q_gain: float32 [2048], replicated, may hold values from 0.5 to 1.5
- k_gain: float32 [2048], replicated, may hold values from 0.5 to 1.5
- w_query: bfloat16 [2048, 2048], P('dp', 'tensor'), may hold values from -0.125 to 0.125
- w_key: bfloat16 [2048, 2048], P('dp', 'tensor'), may hold values from -0.125 to 0.125
- w_value: bfloat16 [2048, 2048], P('dp', 'tensor'), may hold values from -0.125 to 0.125
- w_out: bfloat16 [2048, 2048], P('tensor', 'dp'), may hold values from -1 to 1
- mlp_gain: float32 [2048], replicated, may hold values from 0.5 to 1.5
- router: bfloat16 [2048, 16], replicated, may hold values from -0.0625 to 0.0625
- w_gate: bfloat16 [16, 2048, 1024], P('dp', None, 'tensor'), may hold values from -0.125 to 0.125
- w_up: bfloat16 [16, 2048, 1024], P('dp', None, 'tensor'), may hold values from -0.125 to 0.125
- w_down: bfloat16 [16, 1024, 2048], P('dp', 'tensor'), may hold values from -1.75 to 1.75
Outputs:
- layer_out: bfloat16 [6144, 2048], P(('dp', 'tensor'))
- tokens_grad: float32 [6144, 2048], P(('dp', 'tensor'))
- attn_gain_grad: float32 [2048], replicated
- q_gain_grad: float32 [2048], replicated
- k_gain_grad: float32 [2048], replicated
- w_query_grad: float32 [2048, 2048], P('dp', 'tensor')
- w_key_grad: float32 [2048, 2048], P('dp', 'tensor')
- w_value_grad: float32 [2048, 2048], P('dp', 'tensor')
- w_out_grad: float32 [2048, 2048], P('tensor', 'dp')
- mlp_gain_grad: float32 [2048], replicated
- router_grad: float32 [2048, 16], replicated
- w_gate_grad: float32 [16, 2048, 1024], P('dp', None, 'tensor')
- w_up_grad: float32 [16, 2048, 1024], P('dp', None, 'tensor')
- w_down_grad: float32 [16, 1024, 2048], P('dp', 'tensor')
Inputs may be any that keep to these rules, and one draw needn't show every extreme that they name: `routes`: each row names 8 different experts; in each aligned block of 192 rows no expert is named by more than 128 rows, and in some block one expert is named by exactly 128 rows.
All inputs are finite; a program needn't handle non-finite values.
Results may differ from a plain program's by a relative error of at most 0.018.
Values may be sent and summed in bfloat16 or wider, within the bound.
A program may use at most 320 MiB of HBM per device.

v0:
```python
import jax
import jax.numpy as jnp
from jax import lax
from jax.sharding import PartitionSpec as P

D = 2048
HEAD = 128
TOPK = 8
PROMPT = 256
CONT = 64
GROUP = 384
EPSILON = 1e-05
ROPE_BASE = 10000.0
HIGHEST = lax.Precision.HIGHEST


def matmul(first_op, second_op):
    return jnp.dot(first_op, second_op, preferred_element_type=jnp.float32)


def gather_rows(values):
    return lax.all_gather(values, "tensor", axis=0, tiled=True)


def sum_rows(values):
    return lax.psum_scatter(values, "tensor", scatter_dimension=0, tiled=True)


def tensor_total(values):
    return lax.psum((values[0], values[1]), "tensor")


def expert_swap(values):
    return lax.all_to_all(values, "dp", split_axis=0, concat_axis=0, tiled=True)


def sum_slots(values):
    return lax.psum_scatter(values, "tensor", scatter_dimension=1, tiled=True)


def group_positions():
    position = jnp.arange(GROUP, dtype=jnp.int32)
    return jnp.where(position < PROMPT, position, PROMPT + (position - PROMPT) % CONT)


def visible_keys():
    position = jnp.arange(GROUP, dtype=jnp.int32)
    member = jnp.where(position < PROMPT, -1, (position - PROMPT) // CONT)
    causal = position[None, :] <= position[:, None]
    return causal & ((member[None, :] == -1) | (member[None, :] == member[:, None]))


def rope_tables():
    half_head = HEAD // 2
    frequency = ROPE_BASE ** (-2.0 * jnp.arange(half_head, dtype=jnp.float32) / HEAD)
    angles = group_positions().astype(jnp.float32)[:, None] * frequency[None, :]
    angles = jnp.concatenate([angles, angles], axis=1)
    return (jnp.cos(angles), jnp.sin(angles))


def rotate(values, cosine_table, sine_table):
    half_head = HEAD // 2
    turned = jnp.concatenate([-values[..., half_head:], values[..., :half_head]], axis=-1)
    return values * cosine_table[:, None, :] + turned * sine_table[:, None, :]


def unrotate(values, cosine_table, sine_table):
    half_head = HEAD // 2
    scaled = values * sine_table[:, None, :]
    turned = jnp.concatenate([scaled[..., half_head:], -scaled[..., :half_head]], axis=-1)
    return values * cosine_table[:, None, :] + turned


def gate_split(rows_in, hot_table, router):
    gates = jax.nn.softmax(matmul(rows_in, router), axis=1)
    weights = jnp.sum(jnp.where(hot_table, gates[:, None, :], 0.0), axis=2)
    return (gates, weights)


def body(
    tokens,
    routes,
    cotangent,
    attn_gain,
    q_gain,
    k_gain,
    w_query,
    w_key,
    w_value,
    w_out,
    mlp_gain,
    router,
    w_gate,
    w_up,
    w_down,
):
    rank_index = lax.axis_index("tensor")
    tensor_count = lax.axis_size("tensor")
    own_rows = tokens.shape[0]
    head_cols = w_query.shape[1]
    local_heads = head_cols // HEAD
    col_start = rank_index * head_cols
    row_start = rank_index * own_rows
    experts = router.shape[1]
    half_cap = (own_rows * TOPK * 4 + 3 * experts - 1) // (3 * experts)
    capacity = tensor_count * half_cap
    attn_scale = HEAD ** (-0.5)
    head_shape = (GROUP, local_heads, HEAD)
    q_gain_local = lax.dynamic_slice_in_dim(q_gain, col_start, head_cols)
    k_gain_local = lax.dynamic_slice_in_dim(k_gain, col_start, head_cols)
    inputs = tokens.astype(jnp.float32)
    attn_inv = lax.rsqrt(jnp.mean(inputs * inputs, axis=1, keepdims=True) + EPSILON)
    normed = gather_rows((inputs * attn_inv * attn_gain).astype(jnp.bfloat16))
    pieces = (
        lax.all_gather(w_query, "dp", axis=0, tiled=True),
        lax.all_gather(w_key, "dp", axis=0, tiled=True),
        lax.all_gather(w_value, "dp", axis=0, tiled=True),
    )
    normed_part = normed
    queries = matmul(normed_part, pieces[0])
    keys_raw = matmul(normed_part, pieces[1])
    values_raw = matmul(normed_part, pieces[2])
    query_sq, key_sq = tensor_total(
        (jnp.sum(queries * queries, axis=1), jnp.sum(keys_raw * keys_raw, axis=1))
    )
    query_inv = lax.rsqrt(query_sq / D + EPSILON)[:, None]
    key_inv = lax.rsqrt(key_sq / D + EPSILON)[:, None]
    cosine_table, sine_table = rope_tables()
    query_rot = rotate(
        (queries * query_inv * q_gain_local).reshape(head_shape), cosine_table, sine_table
    ).astype(jnp.bfloat16)
    key_rot = rotate(
        (keys_raw * key_inv * k_gain_local).reshape(head_shape), cosine_table, sine_table
    ).astype(jnp.bfloat16)
    value_heads = values_raw.astype(jnp.bfloat16).reshape(head_shape)
    visible = visible_keys()[None]

    def masked_scores():
        raw_scores = (
            jnp.einsum("qhd,khd->hqk", query_rot, key_rot, preferred_element_type=jnp.float32)
            * attn_scale
        )
        return jnp.where(visible, raw_scores, -1e30)

    scores = masked_scores()
    row_max = jnp.max(scores, axis=2, keepdims=True)
    exponent = jnp.exp(scores - row_max)
    row_total = jnp.sum(exponent, axis=2, keepdims=True)
    log_total = row_max + jnp.log(row_total)
    mixed_heads = jnp.einsum(
        "hqk,khd->qhd",
        (exponent / row_total).astype(jnp.bfloat16),
        value_heads,
        preferred_element_type=jnp.float32,
    )
    mixed_heads = mixed_heads.reshape(GROUP, head_cols).astype(jnp.bfloat16)
    attn_part = matmul(mixed_heads, lax.all_gather(w_out, "dp", axis=1, tiled=True))
    attended = sum_rows(attn_part)
    hidden_one = inputs + attended
    mlp_inv = lax.rsqrt(jnp.mean(hidden_one * hidden_one, axis=1, keepdims=True) + EPSILON)
    normed_two = (hidden_one * mlp_inv * mlp_gain).astype(jnp.bfloat16)
    expert_ids = jnp.arange(experts, dtype=jnp.int32)
    route_hot = routes[:, :, None] == expert_ids[None, None, :]
    flat_hot = route_hot.astype(jnp.int32).reshape(tensor_count, own_rows * TOPK, experts)
    within = jnp.sum((jnp.cumsum(flat_hot, axis=1) - flat_hot) * flat_hot, axis=2).reshape(
        GROUP, TOPK
    )
    owner_of = (jnp.arange(GROUP, dtype=jnp.int32) // own_rows)[:, None]
    own_routes = lax.dynamic_slice_in_dim(routes, row_start, own_rows, 0)
    own_within = lax.dynamic_slice_in_dim(within, row_start, own_rows, 0)
    own_hot = lax.dynamic_slice_in_dim(route_hot, row_start, own_rows, 0)
    own_dest = own_routes * half_cap + own_within
    gate_weight = w_gate[0]
    up_weight = w_up[0]
    down_weight = w_down[0]
    normed_two_all = gather_rows(normed_two)
    gates_every, gate_every = gate_split(normed_two_all, route_hot, router)
    own_probs = lax.dynamic_slice_in_dim(gates_every, row_start, own_rows, 0)
    gate_weights = lax.dynamic_slice_in_dim(gate_every, row_start, own_rows, 0)
    destination = routes * capacity + owner_of * half_cap + within
    send_rows = (
        jnp.zeros((experts * capacity, D), jnp.bfloat16)
        .at[destination]
        .set(jnp.broadcast_to(normed_two_all[:, None, :], (GROUP, TOPK, D)))
        .reshape(experts, capacity, D)
    )
    received = lax.all_to_all(send_rows, "dp", split_axis=0, concat_axis=0, tiled=True)
    gate_pre = jnp.einsum("scd,df->scf", received, gate_weight, preferred_element_type=jnp.float32)
    up_pre = jnp.einsum("scd,df->scf", received, up_weight, preferred_element_type=jnp.float32)
    hidden = (jax.nn.silu(gate_pre) * up_pre).astype(jnp.bfloat16)
    expert_part = jnp.einsum("scf,fd->scd", hidden, down_weight, preferred_element_type=jnp.float32)
    expert_part, gate_pre, up_pre, hidden, received = (
        expert_part,
        gate_pre,
        up_pre,
        hidden,
        received,
    )
    back_rows = expert_swap(sum_slots(expert_part).astype(jnp.bfloat16)).reshape(
        experts * half_cap, D
    )
    picked = back_rows[own_dest].astype(jnp.float32)
    mixture = jnp.sum(gate_weights[:, :, None] * picked, axis=1)
    layer_out = (hidden_one + mixture).astype(jnp.bfloat16)
    upstream = cotangent.astype(jnp.float32)
    gate_grad = jnp.sum(upstream[:, None, :] * picked, axis=2)
    upstream_all = gather_rows(cotangent).astype(jnp.float32)
    send_grads = (
        jnp.zeros((experts * capacity, D), jnp.bfloat16)
        .at[destination]
        .set((gate_every[:, :, None] * upstream_all[:, None, :]).astype(jnp.bfloat16))
        .reshape(experts, capacity, D)
    )
    out_grads = expert_swap(send_grads)
    hidden_grad = jnp.einsum(
        "scd,fd->scf", out_grads, down_weight, preferred_element_type=jnp.float32
    )
    sigmoid = jax.nn.sigmoid(gate_pre)
    up_grad = (hidden_grad * gate_pre * sigmoid).astype(jnp.bfloat16)
    gate_pre_grad = (hidden_grad * up_pre * sigmoid * (1.0 + gate_pre * (1.0 - sigmoid))).astype(
        jnp.bfloat16
    )
    row_part = jnp.einsum(
        "scf,df->scd", gate_pre_grad, gate_weight, preferred_element_type=jnp.float32
    ) + jnp.einsum("scf,df->scd", up_grad, up_weight, preferred_element_type=jnp.float32)
    down_weight_grad = jnp.einsum(
        "scf,scd->fd", hidden, out_grads, preferred_element_type=jnp.float32
    )
    gate_weight_grad = jnp.einsum(
        "scd,scf->df", received, gate_pre_grad, preferred_element_type=jnp.float32
    )
    up_weight_grad = jnp.einsum(
        "scd,scf->df", received, up_grad, preferred_element_type=jnp.float32
    )
    returned_grads = expert_swap(sum_slots(row_part).astype(jnp.bfloat16)).reshape(
        experts * half_cap, D
    )
    normed_two_part = jnp.sum(returned_grads[own_dest].astype(jnp.float32), axis=1)
    expert_grad = jnp.sum(jnp.where(own_hot, gate_grad[:, :, None], 0.0), axis=1)
    logit_grad = own_probs * (expert_grad - jnp.sum(expert_grad * own_probs, axis=1, keepdims=True))
    router_grad = jnp.dot(normed_two.astype(jnp.float32).T, logit_grad, precision=HIGHEST)
    normed_two_grad = normed_two_part + jnp.dot(
        logit_grad, router.astype(jnp.float32).T, precision=HIGHEST
    )
    scaled_grad = normed_two_grad * mlp_gain
    hidden_one_grad = (
        upstream
        + mlp_inv * scaled_grad
        - hidden_one * mlp_inv**3 * jnp.mean(hidden_one * scaled_grad, axis=1, keepdims=True)
    )
    mlp_gain_grad = jnp.sum(normed_two_grad * hidden_one * mlp_inv, axis=0)
    attended_grad = gather_rows(hidden_one_grad.astype(jnp.bfloat16))
    mixed_grad = jnp.einsum(
        "gd,cd->gc",
        attended_grad,
        lax.all_gather(w_out, "dp", axis=1, tiled=True),
        preferred_element_type=jnp.float32,
    )
    mixed_grad = mixed_grad.astype(jnp.bfloat16).reshape(head_shape)
    attn_probs = jnp.exp(masked_scores() - log_total)
    prob_grad = jnp.einsum(
        "qhd,khd->hqk", mixed_grad, value_heads, preferred_element_type=jnp.float32
    )
    row_dot = jnp.sum(prob_grad * attn_probs, axis=2, keepdims=True)
    score_grad = (attn_probs * (prob_grad - row_dot)).astype(jnp.bfloat16)
    query_rot_grad = (
        jnp.einsum("hqk,khd->qhd", score_grad, key_rot, preferred_element_type=jnp.float32)
        * attn_scale
    )
    key_rot_grad = (
        jnp.einsum("hqk,qhd->khd", score_grad, query_rot, preferred_element_type=jnp.float32)
        * attn_scale
    )
    value_grad = (
        jnp.einsum(
            "hqk,qhd->khd",
            attn_probs.astype(jnp.bfloat16),
            mixed_grad,
            preferred_element_type=jnp.float32,
        )
        .reshape(GROUP, head_cols)
        .astype(jnp.bfloat16)
    )
    query_norm_grad = unrotate(query_rot_grad, cosine_table, sine_table).reshape(GROUP, head_cols)
    key_norm_grad = unrotate(key_rot_grad, cosine_table, sine_table).reshape(GROUP, head_cols)
    query_scaled = query_norm_grad * q_gain_local
    key_scaled = key_norm_grad * k_gain_local
    query_dot, key_dot = tensor_total(
        (jnp.sum(queries * query_scaled, axis=1), jnp.sum(keys_raw * key_scaled, axis=1))
    )
    query_grad = (
        query_inv * query_scaled - queries * query_inv**3 * (query_dot / D)[:, None]
    ).astype(jnp.bfloat16)
    key_grad = (key_inv * key_scaled - keys_raw * key_inv**3 * (key_dot / D)[:, None]).astype(
        jnp.bfloat16
    )
    q_gain_part = jnp.sum(query_norm_grad * queries * query_inv, axis=0)
    k_gain_part = jnp.sum(key_norm_grad * keys_raw * key_inv, axis=0)
    pieces = lax.all_gather((w_query, w_key, w_value), "dp", axis=0, tiled=True)
    normed_part = (
        jnp.einsum("gc,rc->gr", query_grad, pieces[0], preferred_element_type=jnp.float32)
        + jnp.einsum("gc,rc->gr", key_grad, pieces[1], preferred_element_type=jnp.float32)
        + jnp.einsum("gc,rc->gr", value_grad, pieces[2], preferred_element_type=jnp.float32)
    )
    weight_sums = lax.psum_scatter(
        jnp.concatenate(
            [
                jnp.einsum("gr,gc->rc", normed, query_grad, preferred_element_type=jnp.float32),
                jnp.einsum("gr,gc->rc", normed, key_grad, preferred_element_type=jnp.float32),
                jnp.einsum("gr,gc->rc", normed, value_grad, preferred_element_type=jnp.float32),
                jnp.einsum(
                    "gr,gc->rc", attended_grad, mixed_heads, preferred_element_type=jnp.float32
                ),
            ],
            axis=1,
        ),
        "dp",
        scatter_dimension=0,
        tiled=True,
    )
    normed_grad = sum_rows(normed_part)
    scaled_input = normed_grad * attn_gain
    tokens_grad = (
        hidden_one_grad
        + attn_inv * scaled_input
        - inputs * attn_inv**3 * jnp.mean(inputs * scaled_input, axis=1, keepdims=True)
    )
    attn_gain_grad = jnp.sum(normed_grad * inputs * attn_inv, axis=0)
    zero_width = jnp.zeros((D,), jnp.float32)
    q_gain_full = lax.dynamic_update_slice_in_dim(zero_width, q_gain_part, col_start, 0)
    k_gain_full = lax.dynamic_update_slice_in_dim(zero_width, k_gain_part, col_start, 0)
    attn_gain_grad, q_gain_grad, k_gain_grad, mlp_gain_grad, router_grad = lax.psum(
        (attn_gain_grad, q_gain_full, k_gain_full, mlp_gain_grad, router_grad), ("dp", "tensor")
    )
    return (
        layer_out,
        tokens_grad,
        attn_gain_grad,
        q_gain_grad,
        k_gain_grad,
        weight_sums[:, :head_cols],
        weight_sums[:, head_cols : 2 * head_cols],
        weight_sums[:, 2 * head_cols : 3 * head_cols],
        jnp.transpose(weight_sums[:, 3 * head_cols :]),
        mlp_gain_grad,
        router_grad,
        gate_weight_grad[None],
        up_weight_grad[None],
        down_weight_grad[None],
    )


def solution(mesh):
    in_specs = (
        P(("dp", "tensor"), None),
        P("dp", None),
        P(("dp", "tensor"), None),
        P(),
        P(),
        P(),
        P("dp", "tensor"),
        P("dp", "tensor"),
        P("dp", "tensor"),
        P("tensor", "dp"),
        P(),
        P(),
        P("dp", None, "tensor"),
        P("dp", None, "tensor"),
        P("dp", "tensor", None),
    )
    out_specs = (
        P(("dp", "tensor"), None),
        P(("dp", "tensor"), None),
        P(),
        P(),
        P(),
        P("dp", "tensor"),
        P("dp", "tensor"),
        P("dp", "tensor"),
        P("tensor", "dp"),
        P(),
        P(),
        P("dp", None, "tensor"),
        P("dp", None, "tensor"),
        P("dp", "tensor", None),
    )
    return jax.shard_map(body, mesh=mesh, in_specs=in_specs, out_specs=out_specs, check_vma=False)
```

profile of v0, /device:TPU:0, one launch (start us, length us, event | category | flops | bytes accessed | tf_op | source)
XLA Modules:
  0.0 2718.6 jit_solution(3922574708786858665)
XLA Ops:
  16.7 25.5 all-gather.9.cloned.1.call-done
  42.2 52.9 %all-gather.15.cloned.1.call-done = bf16[2048,1024]{1,0:T(8,128)(2,1)} async-done(((bf16[128,1024]{1,0:T(8,128)(2,1)}), bf16[2048,1024]{1,0:T(8,128)(2,1)}) %all-gather.15.cloned.1.call-update) | async-done | bytes 4194320 | tf_op jit(solution)/shard_map/all_gather | solution.py:116
  100.7 45.7 %all-gather.13.cloned.1.call-done = bf16[2048,1024]{1,0:T(8,128)(2,1)} async-done(((bf16[128,1024]{1,0:T(8,128)(2,1)}), bf16[2048,1024]{1,0:T(8,128)(2,1)}) %all-gather.13.cloned.1.call-update) | async-done | bytes 4194320 | tf_op jit(solution)/shard_map/all_gather | solution.py:115
  177.6 20.0 all-gather.11.cloned.1.call-done
  204.2 47.0 %all-gather.17.cloned.1.call-done = bf16[1024,2048]{1,0:T(8,128)(2,1)} async-done(((bf16[1024,128]{1,0:T(8,128)(2,1)}), bf16[1024,2048]{1,0:T(8,128)(2,1)}) %all-gather.17.cloned.1.call-update) | async-done | bytes 4194320 | tf_op jit(solution)/shard_map/all_gather | solution.py:157
  257.2 41.4 %reduce-scatter.6.cloned.1.call-done = f32[192,2048]{1,0:T(8,128)} async-done(((f32[384,2048]{1,0:T(8,128)}), f32[192,2048]{1,0:T(8,128)}) %reduce-scatter.6.cloned.1.call-update) | async-done | bytes 1572880 | tf_op jit(solution)/shard_map/reduce_scatter | solution.py:26
  313.4 16.6 all-gather.19.cloned.1.call-done
  330.0 27.6 %scatter_custom_fusion = bf16[4096,2048]{1,0:T(8,128)(2,1)} fusion(s32[3072]{0:T(1024)S(1)} %reshape.372, bf16[]{:T(256)} %constant.98.clone.1, bf16[384,2048]{1,0:T(8,128)(2,1)} %all-gather.19.cloned.1.call-done), kind=kCustom, calls=%fused_computation.14 | custom fusion | bytes 18350082 | tf_op jit(solution)/shard_map/scatter | solution.py:184
  364.1 29.3 %all-gather.21.cloned.1.call-done = bf16[384,2048]{1,0:T(8,128)(2,1)} async-done(((bf16[192,2048]{1,0:T(8,128)(2,1)}), bf16[384,2048]{1,0:T(8,128)(2,1)}) %all-gather.21.cloned.1.call-update) | async-done | bytes 1572880 | tf_op jit(solution)/shard_map/all_gather | solution.py:22
  398.4 28.4 %scatter_custom_fusion.1 = bf16[4096,2048]{1,0:T(8,128)(2,1)} fusion(s32[3072]{0:T(1024)S(1)} %reshape.372, f32[384,2048]{1,0:T(8,128)} %convert_element_type.127, f32[384,8]{1,0:T(8,128)S(1)} %copy.176, bf16[]{:T(256)} %constant.98.clone.1), kind=kCustom, calls=%fused_computation.12 | custom fusion | flops 12582912 | bytes 20119554 | tf_op jit(solution)/shard_map/scatter | solution.py:211
  426.8 233.3 %all-to-all-done = bf16[16,256,2048]{2,1,0:T(8,128)(2,1)} async-done(((bf16[16,256,2048]{2,1,0:T(8,128)(2,1)}), bf16[16,256,2048]{2,1,0:T(8,128)(2,1)}, u32[]{:S(2)}, u32[]{:S(2)}) %all-to-all-start) | async-done | bytes 16777248 | tf_op jit(solution)/shard_map/all_to_all | solution.py:187
  660.1 70.3 %all-to-all-start.2 = ((bf16[16,256,2048]{2,1,0:T(8,128)(2,1)}), bf16[16,256,2048]{2,1,0:T(8,128)(2,1)}, u32[]{:S(2)}, u32[]{:S(2)}) async-start(bf16[16,256,2048]{2,1,0:T(8,128)(2,1)} %bitcast.140), calls=%async_computation.4 | async-start | bytes 33554432 | tf_op jit(solution)/shard_map/all_to_all | solution.py:34
  730.6 15.2 fusion.23
  745.8 14.5 fusion.27
  760.3 266.8 %all-to-all-done.2 = bf16[16,256,2048]{2,1,0:T(8,128)(2,1)} async-done(((bf16[16,256,2048]{2,1,0:T(8,128)(2,1)}), bf16[16,256,2048]{2,1,0:T(8,128)(2,1)}, u32[]{:S(2)}, u32[]{:S(2)}) %all-to-all-start.2) | async-done | bytes 16777248 | tf_op jit(solution)/shard_map/all_to_all | solution.py:34
  1027.2 24.2 multiply_convert_fusion.1
  1051.4 17.9 fusion.25
  1069.3 28.5 %convolution_add_fusion = f32[16,256,2048]{2,1,0:T(8,128)} fusion(f32[16,256,2048]{2,1,0:T(8,128)} %fusion.25, bf16[16,256,512]{2,1,0:T(8,128)(2,1)} %get-tuple-element.106, bf16[1,2048,512]{2,1,0:T(8,128)(2,1)} %param.28), kind=kOutput, calls=%fused_computation.6 | convolution fusion | flops 8598323200 | bytes 73400320 | tf_op jit(solution)/shard_map/scf,df->scd/dot_general | solution.py:225
  1097.8 17.6 fusion.20
  1115.4 416.0 %reduce-scatter.10.cloned.1.call-done = f32[16,128,2048]{2,1,0:T(8,128)} async-done(((f32[16,256,2048]{2,1,0:T(8,128)}), f32[16,128,2048]{2,1,0:T(8,128)}) %reduce-scatter.10.cloned.1.call-update) | async-done | bytes 16777232 | tf_op jit(solution)/shard_map/reduce_scatter | solution.py:38
  1546.2 356.4 %reduce-scatter.8.cloned.1.call-done = f32[16,128,2048]{2,1,0:T(8,128)} async-done(((f32[16,256,2048]{2,1,0:T(8,128)}), f32[16,128,2048]{2,1,0:T(8,128)}) %reduce-scatter.8.cloned.1.call-update) | async-done | bytes 16777232 | tf_op jit(solution)/shard_map/reduce_scatter | solution.py:38
  1919.4 17.3 gather_fusion.1
  1945.6 122.6 %all-to-all-done.1 = bf16[16,128,2048]{2,1,0:T(8,128)(2,1)} async-done(((bf16[16,128,2048]{2,1,0:T(8,128)(2,1)}), bf16[16,128,2048]{2,1,0:T(8,128)(2,1)}, u32[]{:S(2)}, u32[]{:S(2)}) %all-to-all-start.1) | async-done | bytes 8388640 | tf_op jit(solution)/shard_map/all_to_all | solution.py:34
  2068.2 17.1 gather_fusion
  2099.2 58.2 %all-gather.23.cloned.1.call-done = bf16[384,2048]{1,0:T(8,128)(2,1)} async-done(((bf16[192,2048]{1,0:T(8,128)(2,1)}), bf16[384,2048]{1,0:T(8,128)(2,1)}) %all-gather.23.cloned.1.call-update) | async-done | bytes 1572880 | tf_op jit(solution)/shard_map/all_gather | solution.py:22
  2216.1 25.2 pad_maximum_fusion
  2241.6 15.2 convolution_bitcast_fusion
  2256.8 15.6 convolution_bitcast_fusion.1
  2272.4 15.5 convolution_bitcast_fusion.2
  2291.9 42.9 %all-reduce = (f32[2048]{0:T(1024)}, f32[2048]{0:T(1024)}, f32[2048]{0:T(1024)}, f32[2048]{0:T(1024)}) all-reduce(f32[2048]{0:T(1024)S(1)} %get-tuple-element.92, f32[2048]{0:T(1024)S(1)} %dynamic_update_slice.6, f32[2048]{0:T(1024)S(1)} %dynamic_update_slice.7, ...), channel_id=1, replica_groups=mesh['dp'=16,'tensor'=2] {'dp','tensor'}, use_global_device_ids=true, to_apply=%region_33.34 | all-reduce | flops 8192 | bytes 65536 | tf_op jit(solution)/shard_map/psum | solution.py:332
  2338.3 244.4 %reduce-scatter.14.cloned.1.call-done = f32[128,4096]{0,1:T(8,128)} async-done(((f32[2048,4096]{0,1:T(8,128)}), f32[128,4096]{0,1:T(8,128)}) %reduce-scatter.14.cloned.1.call-update) | async-done | bytes 2097168 | tf_op jit(solution)/shard_map/reduce_scatter | solution.py:305
  2589.5 120.7 %all-reduce.5.cloned.1.call-done = f32[2048,16]{0,1:T(8,128)} async-done(((f32[2048,16]{0,1:T(8,128)}), f32[2048,16]{0,1:T(8,128)}) %all-reduce.5.cloned.1.call-update) | async-done | bytes 131088 | tf_op jit(solution)/shard_map/psum | solution.py:332
  (298 shorter events, 213.4 us)
Async XLA Ops:
  7.2 1020.0 %copy-start = (bf16[1,512,2048]{2,1,0:T(8,128)(2,1)S(1)}, bf16[1,512,2048]{2,1,0:T(8,128)(2,1)}, u32[]{:S(2)}) copy-start(bf16[1,512,2048]{2,1,0:T(8,128)(2,1)} %param.29) | copy-start | bytes 6291460
  7.2 35.0 %all-gather.9.cloned.1.call-start = ((), (), s32[]{:S(2)}) async-start(), calls=%async_computation.9 | async-start | bytes 2359296 | tf_op jit(solution)/shard_map/all_gather | solution.py:22
  12.2 83.0 %all-gather.15.cloned.1.call-start = ((), (), s32[]{:S(2)}) async-start(), calls=%async_computation.12 | async-start | bytes 4456448 | tf_op jit(solution)/shard_map/all_gather | solution.py:116
  12.9 133.5 %all-gather.13.cloned.1.call-start = ((), (), s32[]{:S(2)}) async-start(), calls=%async_computation.11 | async-start | bytes 4456448 | tf_op jit(solution)/shard_map/all_gather | solution.py:115
  13.7 183.9 %all-gather.11.cloned.1.call-start = ((), (), s32[]{:S(2)}) async-start(), calls=%async_computation.10 | async-start | bytes 4456448 | tf_op jit(solution)/shard_map/all_gather | solution.py:117
  14.2 237.0 %all-gather.17.cloned.1.call-start = ((), (), s32[]{:S(2)}) async-start(), calls=%async_computation.13 | async-start | bytes 4456448 | tf_op jit(solution)/shard_map/all_gather | solution.py:157
  14.8 283.8 %reduce-scatter.6.cloned.1.call-start = ((), (), s32[]{:S(2)}) async-start(), calls=%async_computation.14 | async-start | bytes 4718592 | tf_op jit(solution)/shard_map/reduce_scatter | solution.py:26
  14.9 149.2 %copy-start.51 = (f32[1024]{0:T(1024)}, f32[1024]{0:T(1024)S(1)}, u32[]{:S(2)}) copy-start(f32[1024]{0:T(1024)S(1)} %dynamic_slice.21) | copy-start | bytes 12292
  14.9 142.8 %copy-start.49 = (f32[1024]{0:T(1024)}, f32[1024]{0:T(1024)S(1)}, u32[]{:S(2)}) copy-start(f32[1024]{0:T(1024)S(1)} %dynamic_slice.22) | copy-start | bytes 12292
  174.8 27.4 %copy-start.42 = (f32[8,384]{1,0:T(8,128)}, f32[8,384]{1,0:T(8,128)S(1)}, u32[]{:S(2)}) copy-start(f32[8,384]{1,0:T(8,128)S(1)} %get-tuple-element.144) | copy-start | bytes 36868
  204.2 47.0 %copy-start.21 = (bf16[8,128,384]{2,1,0:T(8,128)(2,1)}, bf16[8,128,384]{2,1,0:T(8,128)(2,1)S(1)}, u32[]{:S(2)}) copy-start(bf16[8,128,384]{2,1,0:T(8,128)(2,1)S(1)} %fusion.41) | copy-start | bytes 2359300
  256.9 41.7 %copy-start.6 = (bf16[192,2048]{1,0:T(8,128)(2,1)S(1)}, bf16[192,2048]{1,0:T(8,128)(2,1)}, u32[]{:S(2)}) copy-start(bf16[192,2048]{1,0:T(8,128)(2,1)} %param.15) | copy-start | bytes 2359300
  257.0 44.6 %copy-start.47 = (f32[2048]{0:T(1024)S(1)}, f32[2048]{0:T(1024)}, u32[]{:S(2)}) copy-start(f32[2048]{0:T(1024)} %param.25) | copy-start | bytes 24580
  257.0 73.1 %all-gather.19.cloned.1.call-start = ((), (), s32[]{:S(2)}) async-start(), calls=%async_computation.15 | async-start | bytes 2359296 | tf_op jit(solution)/shard_map/all_gather | solution.py:22
  302.8 54.9 %copy-start.28 = (s32[384,8]{1,0:T(8,128)}, s32[384,8]{1,0:T(8,128)S(1)}, u32[]{:S(2)}) copy-start(s32[384,8]{1,0:T(8,128)S(1)} %copy.169) | copy-start | bytes 36868
  313.1 44.6 %copy-start.30 = (s32[384,8]{1,0:T(8,128)}, s32[384,8]{1,0:T(8,128)S(1)}, u32[]{:S(2)}) copy-start(s32[384,8]{1,0:T(8,128)S(1)} %reshape.346) | copy-start | bytes 36868
  357.7 302.4 %all-to-all-start = ((bf16[16,256,2048]{2,1,0:T(8,128)(2,1)}), bf16[16,256,2048]{2,1,0:T(8,128)(2,1)}, u32[]{:S(2)}, u32[]{:S(2)}) async-start(bf16[16,256,2048]{2,1,0:T(8,128)(2,1)} %bitcast.139), calls=%async_computation.1 | async-start | bytes 33554432 | tf_op jit(solution)/shard_map/all_to_all | solution.py:187
  363.4 30.1 %all-gather.21.cloned.1.call-start = ((), (), s32[]{:S(2)}) async-start(), calls=%async_computation.17 | async-start | bytes 2359296 | tf_op jit(solution)/shard_map/all_gather | solution.py:22
  364.1 32.9 %copy-start.38 = (bf16[2048,16]{0,1:T(8,128)(2,1)S(1)}, bf16[2048,16]{0,1:T(8,128)(2,1)}, u32[]{:S(2)}) copy-start(bf16[2048,16]{0,1:T(8,128)(2,1)} %param.26) | copy-start | bytes 196612
  398.3 28.5 %copy-start.44 = (f32[384,8]{0,1:T(8,128)}, f32[384,8]{0,1:T(8,128)S(1)}, u32[]{:S(2)}) copy-start(f32[384,8]{0,1:T(8,128)S(1)} %select_reduce_fusion) | copy-start | bytes 36868
  660.1 367.0 %all-to-all-start.2 = ((bf16[16,256,2048]{2,1,0:T(8,128)(2,1)}), bf16[16,256,2048]{2,1,0:T(8,128)(2,1)}, u32[]{:S(2)}, u32[]{:S(2)}) async-start(bf16[16,256,2048]{2,1,0:T(8,128)(2,1)} %bitcast.140), calls=%async_computation.4 | async-start | bytes 33554432 | tf_op jit(solution)/shard_map/all_to_all | solution.py:34
  730.4 801.0 %reduce-scatter.10.cloned.1.call-start = ((), (), s32[]{:S(2)}) async-start(), calls=%async_computation.18 | async-start | bytes 50331648 | tf_op jit(solution)/shard_map/reduce_scatter | solution.py:38
  1097.8 804.9 %reduce-scatter.8.cloned.1.call-start = ((), (), s32[]{:S(2)}) async-start(), calls=%async_computation.16 | async-start | bytes 50331648 | tf_op jit(solution)/shard_map/reduce_scatter | solution.py:38
  1540.6 371.2 %all-to-all-start.3 = ((bf16[16,128,2048]{2,1,0:T(8,128)(2,1)}), bf16[16,128,2048]{2,1,0:T(8,128)(2,1)}, u32[]{:S(2)}, u32[]{:S(2)}) async-start(bf16[16,128,2048]{2,1,0:T(8,128)(2,1)} %convert_element_type.131), calls=%async_computation.6 | async-start | bytes 16777216 | tf_op jit(solution)/shard_map/all_to_all | solution.py:34
  1911.7 156.5 %all-to-all-start.1 = ((bf16[16,128,2048]{2,1,0:T(8,128)(2,1)}), bf16[16,128,2048]{2,1,0:T(8,128)(2,1)}, u32[]{:S(2)}, u32[]{:S(2)}) async-start(bf16[16,128,2048]{2,1,0:T(8,128)(2,1)} %convert_element_type.123), calls=%async_computation.3 | async-start | bytes 16777216 | tf_op jit(solution)/shard_map/all_to_all | solution.py:34
  1917.6 239.8 %all-gather.23.cloned.1.call-start = ((), (), s32[]{:S(2)}) async-start(), calls=%async_computation.19 | async-start | bytes 2359296 | tf_op jit(solution)/shard_map/all_gather | solution.py:22
  2099.1 190.5 %reduce-scatter.12.cloned.1.call-start = ((), (), s32[]{:S(2)}) async-start(), calls=%async_computation.20 | async-start | bytes 4718592 | tf_op jit(solution)/shard_map/reduce_scatter | solution.py:26
  2165.6 31.9 %copy-start.26 = (bf16[8,128,384]{2,1,0:T(8,128)(2,1)}, bf16[8,128,384]{2,1,0:T(8,128)(2,1)S(1)}, u32[]{:S(2)}) copy-start(bf16[8,128,384]{2,1,0:T(8,128)(2,1)S(1)} %fusion.42) | copy-start | bytes 2359300
  2201.5 381.2 %reduce-scatter.14.cloned.1.call-start = ((), (), s32[]{:S(2)}) async-start(), calls=%async_computation.21 | async-start | bytes 35651584 | tf_op jit(solution)/shard_map/reduce_scatter | solution.py:305
  2241.3 468.9 %all-reduce.5.cloned.1.call-start = ((), (), s32[]{:S(2)}) async-start(), calls=%async_computation.22 | async-start | bytes 262144 | tf_op jit(solution)/shard_map/psum | solution.py:332
  2287.9 46.8 %copy-start.66 = (f32[192]{0:T(256)S(1)}, f32[192]{0:T(256)}, u32[]{:S(2)}) copy-start(f32[192]{0:T(256)} %get-tuple-element.136) | copy-start | bytes 2308
  2582.7 129.1 %copy-start.1 = (bf16[1,512,2048]{2,1,0:T(8,128)(2,1)S(1)}, bf16[1,512,2048]{2,1,0:T(8,128)(2,1)}, u32[]{:S(2)}) copy-start(bf16[1,512,2048]{2,1,0:T(8,128)(2,1)} %param.29) | copy-start | bytes 6291460
  (62 other events, 335.2 us)
Sparse Core Ops, SparseCore 0:
  12.3 29.8 all-gather.8
  44.4 50.7 all-gather.14
  97.3 49.0 all-gather.12
  148.4 49.0 all-gather.10
  199.5 51.7 all-gather.16
  257.1 41.5 reduce-scatter.5
  302.8 27.2 all-gather.18
  365.8 27.5 all-gather.20
  1097.9 433.5 reduce-scatter.9
  1533.7 368.9 reduce-scatter.7
  2099.3 58.0 all-gather.22
  2201.6 43.3 reduce-scatter.11
  2249.2 333.4 reduce-scatter.13
  2588.7 121.4 all-reduce.4
where the time goes:
time: 2720 us
  waiting for transfers between devices  2100 us (77%)
  matrix products  227 us (8%)
  other arithmetic  141 us (5%)
  local copies, waits for them, and re-layouts  93.5 us (3%)
  starting transfers between devices  88.9 us (3%)
  blocking collectives  53.1 us (2%)
    reduce_scatter x2, waiting for transfers between devices, sum_slots(): return lax.psum_scatter(values, 'tensor', scatter_dimension=1, tiled=True)  772 us
    all_to_all x3, waiting for transfers between devices, expert_swap(): return lax.all_to_all(values, 'dp', split_axis=0, concat_axis=0, tiled=True)  389 us
    reduce_scatter x1, waiting for transfers between devices, body(): lax.psum_scatter(jnp.concatenate([jnp.einsum('gr,gc->rc', normed, query_g...  244 us
    all_to_all x1, waiting for transfers between devices, body(): lax.all_to_all(send_rows, 'dp', split_axis=0, concat_axis=0, tiled=True)  233 us
    all_gather x4, waiting for transfers between devices, gather_rows(): return lax.all_gather(values, 'tensor', axis=0, tiled=True)  130 us
    psum x1, waiting for transfers between devices, body(): lax.psum((attn_gain_grad, q_gain_full, k_gain_full, mlp_gain_grad, router...  121 us
    all_to_all x3, starting transfers between devices, expert_swap(): return lax.all_to_all(values, 'dp', split_axis=0, concat_axis=0, tiled=True)  81.7 us
  transfers between devices with their start and end apart: 18, of which 16 were waited for; matrix products, arithmetic and copies ran while one was open for 10% of the time, Pallas kernels for 0%

commit v1 on v0

--- a/solution.py
+++ b/solution.py
@@ -330,7 +330,8 @@
     q_gain_full = lax.dynamic_update_slice_in_dim(zero_width, q_gain_part, col_start, 0)
     k_gain_full = lax.dynamic_update_slice_in_dim(zero_width, k_gain_part, col_start, 0)
     attn_gain_grad, q_gain_grad, k_gain_grad, mlp_gain_grad, router_grad = lax.psum(
-        (attn_gain_grad, q_gain_full, k_gain_full, mlp_gain_grad, router_grad), ("dp", "tensor")
+        lax.psum((attn_gain_grad, q_gain_full, k_gain_full, mlp_gain_grad, router_grad), "tensor"),
+        "dp",
     )
     return (
         layer_out,

time: 2720 us -> 2690 us (0.989)
  waiting for transfers between devices: 2100 us -> 2030 us
  blocking collectives: 53.1 us -> 80.8 us
    psum x1, waiting for transfers between devices: 121 us -> 0.01 us  [body(): lax.psum((attn_gain_grad, q_gain_full, k_gain_full, mlp_gain_grad, router...]
    psum x0 -> x1, waiting for transfers between devices: none -> 82.6 us  [body(): lax.psum(lax.psum((attn_gain_grad, q_gain_full, k_gain_full, mlp_gain_gra...]
    psum x0 -> x1, blocking collectives: none -> 62.6 us  [body(): lax.psum(lax.psum((attn_gain_grad, q_gain_full, k_gain_full, mlp_gain_gra...]
    psum x1, blocking collectives: 42.9 us -> 7.74 us  [body(): lax.psum((attn_gain_grad, q_gain_full, k_gain_full, mlp_gain_grad, router...]
    reduce_scatter x1, waiting for transfers between devices: 244 us -> 217 us  [body(): lax.psum_scatter(jnp.concatenate([jnp.einsum('gr,gc->rc', normed, query_g...]
  transfers between devices with their start and end apart: 18 -> 19, of which waited for: 16 -> 16; matrix products, arithmetic and copies ran while one was open for 10% -> 12% of each run, Pallas kernels for 0% -> 0%
where the time goes in v1:
time: 2690 us; the launch traced here: 2680 us
  waiting for transfers between devices  2030 us (75%)
  matrix products  228 us (8%)
  other arithmetic  141 us (5%)
  local copies, waits for them, and re-layouts  93.5 us (3%)
  starting transfers between devices  89.1 us (3%)
  blocking collectives  80.8 us (3%)
    reduce_scatter x2, waiting for transfers between devices, sum_slots(): return lax.psum_scatter(values, 'tensor', scatter_dimension=1, tiled=True)  773 us
    all_to_all x3, waiting for transfers between devices, expert_swap(): return lax.all_to_all(values, 'dp', split_axis=0, concat_axis=0, tiled=True)  390 us
    all_to_all x1, waiting for transfers between devices, body(): lax.all_to_all(send_rows, 'dp', split_axis=0, concat_axis=0, tiled=True)  233 us
    reduce_scatter x1, waiting for transfers between devices, body(): lax.psum_scatter(jnp.concatenate([jnp.einsum('gr,gc->rc', normed, query_g...  217 us
    all_gather x4, waiting for transfers between devices, gather_rows(): return lax.all_gather(values, 'tensor', axis=0, tiled=True)  127 us
    psum x1, waiting for transfers between devices, body(): lax.psum(lax.psum((attn_gain_grad, q_gain_full, k_gain_full, mlp_gain_gra...  82.6 us
    all_to_all x3, starting transfers between devices, expert_swap(): return lax.all_to_all(values, 'dp', split_axis=0, concat_axis=0, tiled=True)  81.7 us
    psum x1, blocking collectives, body(): lax.psum(lax.psum((attn_gain_grad, q_gain_full, k_gain_full, mlp_gain_gra...  62.6 us
  transfers between devices with their start and end apart: 19, of which 16 were waited for; matrix products, arithmetic and copies ran while one was open for 12% of the time, Pallas kernels for 0%

profile of v1, /device:TPU:0, one launch (start us, length us, event | category | flops | bytes accessed | tf_op | source)
XLA Modules:
  0.0 2679.4 jit_solution(13397387430539216478)
XLA Ops:
  16.7 25.5 all-gather.9.cloned.1.call-done
  42.2 52.9 %all-gather.15.cloned.1.call-done = bf16[2048,1024]{1,0:T(8,128)(2,1)} async-done(((bf16[128,1024]{1,0:T(8,128)(2,1)}), bf16[2048,1024]{1,0:T(8,128)(2,1)}) %all-gather.15.cloned.1.call-update) | async-done | bytes 4194320 | tf_op jit(solution)/shard_map/all_gather | solution.py:116
  100.7 45.7 %all-gather.13.cloned.1.call-done = bf16[2048,1024]{1,0:T(8,128)(2,1)} async-done(((bf16[128,1024]{1,0:T(8,128)(2,1)}), bf16[2048,1024]{1,0:T(8,128)(2,1)}) %all-gather.13.cloned.1.call-update) | async-done | bytes 4194320 | tf_op jit(solution)/shard_map/all_gather | solution.py:115
  177.5 19.9 all-gather.11.cloned.1.call-done
  204.2 47.1 %all-gather.17.cloned.1.call-done = bf16[1024,2048]{1,0:T(8,128)(2,1)} async-done(((bf16[1024,128]{1,0:T(8,128)(2,1)}), bf16[1024,2048]{1,0:T(8,128)(2,1)}) %all-gather.17.cloned.1.call-update) | async-done | bytes 4194320 | tf_op jit(solution)/shard_map/all_gather | solution.py:157
  257.2 41.4 %reduce-scatter.6.cloned.1.call-done = f32[192,2048]{1,0:T(8,128)} async-done(((f32[384,2048]{1,0:T(8,128)}), f32[192,2048]{1,0:T(8,128)}) %reduce-scatter.6.cloned.1.call-update) | async-done | bytes 1572880 | tf_op jit(solution)/shard_map/reduce_scatter | solution.py:26
  313.4 16.6 all-gather.19.cloned.1.call-done
  330.0 27.6 %scatter_custom_fusion = bf16[4096,2048]{1,0:T(8,128)(2,1)} fusion(s32[3072]{0:T(1024)S(1)} %reshape.372, bf16[]{:T(256)} %constant.98.clone.1, bf16[384,2048]{1,0:T(8,128)(2,1)} %all-gather.19.cloned.1.call-done), kind=kCustom, calls=%fused_computation.14 | custom fusion | bytes 18350082 | tf_op jit(solution)/shard_map/scatter | solution.py:184
  364.1 29.3 %all-gather.21.cloned.1.call-done = bf16[384,2048]{1,0:T(8,128)(2,1)} async-done(((bf16[192,2048]{1,0:T(8,128)(2,1)}), bf16[384,2048]{1,0:T(8,128)(2,1)}) %all-gather.21.cloned.1.call-update) | async-done | bytes 1572880 | tf_op jit(solution)/shard_map/all_gather | solution.py:22
  398.4 28.4 %scatter_custom_fusion.1 = bf16[4096,2048]{1,0:T(8,128)(2,1)} fusion(s32[3072]{0:T(1024)S(1)} %reshape.372, f32[384,2048]{1,0:T(8,128)} %convert_element_type.127, f32[384,8]{1,0:T(8,128)S(1)} %copy.176, bf16[]{:T(256)} %constant.98.clone.1), kind=kCustom, calls=%fused_computation.12 | custom fusion | flops 12582912 | bytes 20119554 | tf_op jit(solution)/shard_map/scatter | solution.py:211
  426.8 233.3 %all-to-all-done = bf16[16,256,2048]{2,1,0:T(8,128)(2,1)} async-done(((bf16[16,256,2048]{2,1,0:T(8,128)(2,1)}), bf16[16,256,2048]{2,1,0:T(8,128)(2,1)}, u32[]{:S(2)}, u32[]{:S(2)}) %all-to-all-start) | async-done | bytes 16777248 | tf_op jit(solution)/shard_map/all_to_all | solution.py:187
  660.1 70.3 %all-to-all-start.2 = ((bf16[16,256,2048]{2,1,0:T(8,128)(2,1)}), bf16[16,256,2048]{2,1,0:T(8,128)(2,1)}, u32[]{:S(2)}, u32[]{:S(2)}) async-start(bf16[16,256,2048]{2,1,0:T(8,128)(2,1)} %bitcast.140), calls=%async_computation.4 | async-start | bytes 33554432 | tf_op jit(solution)/shard_map/all_to_all | solution.py:34
  730.6 15.2 fusion.23
  745.8 14.4 fusion.27
  760.2 266.9 %all-to-all-done.2 = bf16[16,256,2048]{2,1,0:T(8,128)(2,1)} async-done(((bf16[16,256,2048]{2,1,0:T(8,128)(2,1)}), bf16[16,256,2048]{2,1,0:T(8,128)(2,1)}, u32[]{:S(2)}, u32[]{:S(2)}) %all-to-all-start.2) | async-done | bytes 16777248 | tf_op jit(solution)/shard_map/all_to_all | solution.py:34
  1027.1 24.2 multiply_convert_fusion.1
  1051.3 17.8 fusion.25
  1069.1 28.5 %convolution_add_fusion = f32[16,256,2048]{2,1,0:T(8,128)} fusion(f32[16,256,2048]{2,1,0:T(8,128)} %fusion.25, bf16[16,256,512]{2,1,0:T(8,128)(2,1)} %get-tuple-element.110, bf16[1,2048,512]{2,1,0:T(8,128)(2,1)} %param.28), kind=kOutput, calls=%fused_computation.6 | convolution fusion | flops 8598323200 | bytes 73400320 | tf_op jit(solution)/shard_map/scf,df->scd/dot_general | solution.py:225
  1097.6 17.5 fusion.20
  1115.1 416.2 %reduce-scatter.10.cloned.1.call-done = f32[16,128,2048]{2,1,0:T(8,128)} async-done(((f32[16,256,2048]{2,1,0:T(8,128)}), f32[16,128,2048]{2,1,0:T(8,128)}) %reduce-scatter.10.cloned.1.call-update) | async-done | bytes 16777232 | tf_op jit(solution)/shard_map/reduce_scatter | solution.py:38
  1546.1 356.4 %reduce-scatter.8.cloned.1.call-done = f32[16,128,2048]{2,1,0:T(8,128)} async-done(((f32[16,256,2048]{2,1,0:T(8,128)}), f32[16,128,2048]{2,1,0:T(8,128)}) %reduce-scatter.8.cloned.1.call-update) | async-done | bytes 16777232 | tf_op jit(solution)/shard_map/reduce_scatter | solution.py:38
  1919.2 17.3 gather_fusion.1
  1945.4 122.6 %all-to-all-done.1 = bf16[16,128,2048]{2,1,0:T(8,128)(2,1)} async-done(((bf16[16,128,2048]{2,1,0:T(8,128)(2,1)}), bf16[16,128,2048]{2,1,0:T(8,128)(2,1)}, u32[]{:S(2)}, u32[]{:S(2)}) %all-to-all-start.1) | async-done | bytes 8388640 | tf_op jit(solution)/shard_map/all_to_all | solution.py:34
  2068.1 17.1 gather_fusion
  2101.4 55.8 %all-gather.23.cloned.1.call-done = bf16[384,2048]{1,0:T(8,128)(2,1)} async-done(((bf16[192,2048]{1,0:T(8,128)(2,1)}), bf16[384,2048]{1,0:T(8,128)(2,1)}) %all-gather.23.cloned.1.call-update) | async-done | bytes 1572880 | tf_op jit(solution)/shard_map/all_gather | solution.py:22
  2216.3 25.1 pad_maximum_fusion
  2241.8 15.2 convolution_bitcast_fusion
  2257.0 15.6 convolution_bitcast_fusion.1
  2272.6 15.4 convolution_bitcast_fusion.2
  2298.5 62.6 %all-reduce = (f32[2048]{0:T(1024)}, f32[2048]{0:T(1024)}, f32[2048]{0:T(1024)}, f32[2048]{0:T(1024)}) all-reduce(f32[2048]{0:T(1024)S(1)} %get-tuple-element.98, f32[2048]{0:T(1024)S(1)} %get-tuple-element.99, f32[2048]{0:T(1024)S(1)} %get-tuple-element.100, ...), channel_id=1, replica_groups=mesh['dp'=16,'tensor'=2] {'dp'}, use_global_device_ids=true, to_apply=%region_34.35 | all-reduce | flops 8192 | bytes 65536 | tf_op jit(solution)/shard_map/psum | solution.py:332
  2364.6 217.1 %reduce-scatter.14.cloned.1.call-done = f32[128,4096]{0,1:T(8,128)} async-done(((f32[2048,4096]{0,1:T(8,128)}), f32[128,4096]{0,1:T(8,128)}) %reduce-scatter.14.cloned.1.call-update) | async-done | bytes 2097168 | tf_op jit(solution)/shard_map/reduce_scatter | solution.py:305
  2588.5 82.6 %all-reduce.9.cloned.1.call-done = f32[2048,16]{0,1:T(8,128)} async-done(((f32[2048,16]{0,1:T(8,128)}), f32[2048,16]{0,1:T(8,128)}) %all-reduce.9.cloned.1.call-update) | async-done | bytes 131088 | tf_op jit(solution)/shard_map/psum | solution.py:332
  (300 shorter events, 222.6 us)
Async XLA Ops:
  7.2 1019.9 %copy-start = (bf16[1,512,2048]{2,1,0:T(8,128)(2,1)S(1)}, bf16[1,512,2048]{2,1,0:T(8,128)(2,1)}, u32[]{:S(2)}) copy-start(bf16[1,512,2048]{2,1,0:T(8,128)(2,1)} %param.29) | copy-start | bytes 6291460
  7.2 35.0 %all-gather.9.cloned.1.call-start = ((), (), s32[]{:S(2)}) async-start(), calls=%async_computation.9 | async-start | bytes 2359296 | tf_op jit(solution)/shard_map/all_gather | solution.py:22
  12.1 83.0 %all-gather.15.cloned.1.call-start = ((), (), s32[]{:S(2)}) async-start(), calls=%async_computation.12 | async-start | bytes 4456448 | tf_op jit(solution)/shard_map/all_gather | solution.py:116
  12.9 133.5 %all-gather.13.cloned.1.call-start = ((), (), s32[]{:S(2)}) async-start(), calls=%async_computation.11 | async-start | bytes 4456448 | tf_op jit(solution)/shard_map/all_gather | solution.py:115
  13.6 183.9 %all-gather.11.cloned.1.call-start = ((), (), s32[]{:S(2)}) async-start(), calls=%async_computation.10 | async-start | bytes 4456448 | tf_op jit(solution)/shard_map/all_gather | solution.py:117
  14.2 237.0 %all-gather.17.cloned.1.call-start = ((), (), s32[]{:S(2)}) async-start(), calls=%async_computation.13 | async-start | bytes 4456448 | tf_op jit(solution)/shard_map/all_gather | solution.py:157
  14.8 283.8 %reduce-scatter.6.cloned.1.call-start = ((), (), s32[]{:S(2)}) async-start(), calls=%async_computation.14 | async-start | bytes 4718592 | tf_op jit(solution)/shard_map/reduce_scatter | solution.py:26
  14.9 149.2 %copy-start.50 = (f32[1024]{0:T(1024)}, f32[1024]{0:T(1024)S(1)}, u32[]{:S(2)}) copy-start(f32[1024]{0:T(1024)S(1)} %dynamic_slice.21) | copy-start | bytes 12292
  14.9 142.8 %copy-start.48 = (f32[1024]{0:T(1024)}, f32[1024]{0:T(1024)S(1)}, u32[]{:S(2)}) copy-start(f32[1024]{0:T(1024)S(1)} %dynamic_slice.22) | copy-start | bytes 12292
  204.2 47.1 %copy-start.20 = (bf16[8,128,384]{2,1,0:T(8,128)(2,1)}, bf16[8,128,384]{2,1,0:T(8,128)(2,1)S(1)}, u32[]{:S(2)}) copy-start(bf16[8,128,384]{2,1,0:T(8,128)(2,1)S(1)} %fusion.41) | copy-start | bytes 2359300
  256.9 41.7 %copy-start.6 = (bf16[192,2048]{1,0:T(8,128)(2,1)S(1)}, bf16[192,2048]{1,0:T(8,128)(2,1)}, u32[]{:S(2)}) copy-start(bf16[192,2048]{1,0:T(8,128)(2,1)} %param.15) | copy-start | bytes 2359300
  256.9 44.6 %copy-start.46 = (f32[2048]{0:T(1024)S(1)}, f32[2048]{0:T(1024)}, u32[]{:S(2)}) copy-start(f32[2048]{0:T(1024)} %param.25) | copy-start | bytes 24580
  256.9 73.1 %all-gather.19.cloned.1.call-start = ((), (), s32[]{:S(2)}) async-start(), calls=%async_computation.15 | async-start | bytes 2359296 | tf_op jit(solution)/shard_map/all_gather | solution.py:22
  302.8 54.9 %copy-start.27 = (s32[384,8]{1,0:T(8,128)}, s32[384,8]{1,0:T(8,128)S(1)}, u32[]{:S(2)}) copy-start(s32[384,8]{1,0:T(8,128)S(1)} %copy.169) | copy-start | bytes 36868
  313.0 44.6 %copy-start.29 = (s32[384,8]{1,0:T(8,128)}, s32[384,8]{1,0:T(8,128)S(1)}, u32[]{:S(2)}) copy-start(s32[384,8]{1,0:T(8,128)S(1)} %reshape.346) | copy-start | bytes 36868
  357.6 302.4 %all-to-all-start = ((bf16[16,256,2048]{2,1,0:T(8,128)(2,1)}), bf16[16,256,2048]{2,1,0:T(8,128)(2,1)}, u32[]{:S(2)}, u32[]{:S(2)}) async-start(bf16[16,256,2048]{2,1,0:T(8,128)(2,1)} %bitcast.139), calls=%async_computation.1 | async-start | bytes 33554432 | tf_op jit(solution)/shard_map/all_to_all | solution.py:187
  363.3 30.1 %all-gather.21.cloned.1.call-start = ((), (), s32[]{:S(2)}) async-start(), calls=%async_computation.17 | async-start | bytes 2359296 | tf_op jit(solution)/shard_map/all_gather | solution.py:22
  364.1 32.9 %copy-start.37 = (bf16[2048,16]{0,1:T(8,128)(2,1)S(1)}, bf16[2048,16]{0,1:T(8,128)(2,1)}, u32[]{:S(2)}) copy-start(bf16[2048,16]{0,1:T(8,128)(2,1)} %param.26) | copy-start | bytes 196612
  398.2 28.5 %copy-start.43 = (f32[384,8]{0,1:T(8,128)}, f32[384,8]{0,1:T(8,128)S(1)}, u32[]{:S(2)}) copy-start(f32[384,8]{0,1:T(8,128)S(1)} %select_reduce_fusion) | copy-start | bytes 36868
  660.1 367.0 %all-to-all-start.2 = ((bf16[16,256,2048]{2,1,0:T(8,128)(2,1)}), bf16[16,256,2048]{2,1,0:T(8,128)(2,1)}, u32[]{:S(2)}, u32[]{:S(2)}) async-start(bf16[16,256,2048]{2,1,0:T(8,128)(2,1)} %bitcast.140), calls=%async_computation.4 | async-start | bytes 33554432 | tf_op jit(solution)/shard_map/all_to_all | solution.py:34
  730.4 800.9 %reduce-scatter.10.cloned.1.call-start = ((), (), s32[]{:S(2)}) async-start(), calls=%async_computation.18 | async-start | bytes 50331648 | tf_op jit(solution)/shard_map/reduce_scatter | solution.py:38
  1097.6 804.9 %reduce-scatter.8.cloned.1.call-start = ((), (), s32[]{:S(2)}) async-start(), calls=%async_computation.16 | async-start | bytes 50331648 | tf_op jit(solution)/shard_map/reduce_scatter | solution.py:38
  1540.4 371.2 %all-to-all-start.3 = ((bf16[16,128,2048]{2,1,0:T(8,128)(2,1)}), bf16[16,128,2048]{2,1,0:T(8,128)(2,1)}, u32[]{:S(2)}, u32[]{:S(2)}) async-start(bf16[16,128,2048]{2,1,0:T(8,128)(2,1)} %convert_element_type.131), calls=%async_computation.6 | async-start | bytes 16777216 | tf_op jit(solution)/shard_map/all_to_all | solution.py:34
  1911.5 156.5 %all-to-all-start.1 = ((bf16[16,128,2048]{2,1,0:T(8,128)(2,1)}), bf16[16,128,2048]{2,1,0:T(8,128)(2,1)}, u32[]{:S(2)}, u32[]{:S(2)}) async-start(bf16[16,128,2048]{2,1,0:T(8,128)(2,1)} %convert_element_type.123), calls=%async_computation.3 | async-start | bytes 16777216 | tf_op jit(solution)/shard_map/all_to_all | solution.py:34
  1917.4 239.8 %all-gather.23.cloned.1.call-start = ((), (), s32[]{:S(2)}) async-start(), calls=%async_computation.19 | async-start | bytes 2359296 | tf_op jit(solution)/shard_map/all_gather | solution.py:22
  2098.9 189.1 %all-reduce.7.cloned.1.call-start = ((), (), s32[]{:S(2)}) async-start(), calls=%async_computation.22 | async-start | bytes 262144 | tf_op jit(solution)/shard_map/psum | solution.py:333
  2101.3 187.3 %reduce-scatter.12.cloned.1.call-start = ((), (), s32[]{:S(2)}) async-start(), calls=%async_computation.20 | async-start | bytes 4718592 | tf_op jit(solution)/shard_map/reduce_scatter | solution.py:26
  2165.4 32.2 %copy-start.25 = (bf16[8,128,384]{2,1,0:T(8,128)(2,1)}, bf16[8,128,384]{2,1,0:T(8,128)(2,1)S(1)}, u32[]{:S(2)}) copy-start(bf16[8,128,384]{2,1,0:T(8,128)(2,1)S(1)} %fusion.42) | copy-start | bytes 2359300
  2201.6 380.2 %reduce-scatter.14.cloned.1.call-start = ((), (), s32[]{:S(2)}) async-start(), calls=%async_computation.21 | async-start | bytes 35651584 | tf_op jit(solution)/shard_map/reduce_scatter | solution.py:305
  2241.5 429.6 %all-reduce.9.cloned.1.call-start = ((), (), s32[]{:S(2)}) async-start(), calls=%async_computation.23 | async-start | bytes 262144 | tf_op jit(solution)/shard_map/psum | solution.py:332
  2288.0 73.2 %copy-start.65 = (f32[192]{0:T(256)S(1)}, f32[192]{0:T(256)}, u32[]{:S(2)}) copy-start(f32[192]{0:T(256)} %get-tuple-element.140) | copy-start | bytes 2308
  2581.7 90.9 %copy-start.1 = (bf16[1,512,2048]{2,1,0:T(8,128)(2,1)S(1)}, bf16[1,512,2048]{2,1,0:T(8,128)(2,1)}, u32[]{:S(2)}) copy-start(bf16[1,512,2048]{2,1,0:T(8,128)(2,1)} %param.29) | copy-start | bytes 6291460
  (62 other events, 343.7 us)
Sparse Core Ops, SparseCore 0:
  12.2 29.8 all-gather.8
  44.4 50.7 all-gather.14
  97.3 49.0 all-gather.12
  148.4 49.0 all-gather.10
  199.5 51.7 all-gather.16
  257.1 41.5 reduce-scatter.5
  302.7 27.2 all-gather.18
  365.8 27.5 all-gather.20
  1097.7 433.5 reduce-scatter.9
  1533.5 368.8 reduce-scatter.7
  2099.0 58.0 all-gather.22
  2160.0 21.4 all-reduce.6
  2201.7 43.3 reduce-scatter.11
  2249.2 332.4 reduce-scatter.13
  2585.0 86.0 all-reduce.8
